TPU v7x, 128 devices: a whole 4x4x4 slice. The times are simulated.
128 devices in a mesh: row: 16 (over x, z), col: 8 (over y, core).
Axes of the slice: x: 4, y: 4, z: 4, core: 2. Of those that a mesh axis runs over, the one named last changes fastest.
Arguments:
- child_tiles: float32 [1024, 256, 256], P(('row', 'col')), may hold values from -2 to 2
- tile_dest: int32 [1024, 2], P(('row', 'col')), may hold values from 0 to 31, as said below
- tile_counts: int32 [16, 8], P('row', 'col'), may hold values from 4 to 8
- child_offsets: int32 [4], replicated, may hold values from 0 to 16
Outputs:
- r_top: float32 [1024, 8192], P(None, 'col')
Inputs may be any that keep to these rules, and one draw needn't show every extreme that they name: tile_dest[t, 0] is a column tile of the front and tile_dest[t, 1] is below 7. Among the 8 slots of one count entry, at most 2 name column tiles of one block of 4 consecutive column tiles (blocks start at multiples of 4); some entry reaches 2 for some block, and some block receives 2 live slots from every entry that shares a row offset residue.
All inputs are finite; a program needn't handle non-finite values.
Results may differ from a plain program's by a relative error of at most 0.00008.
Values sent between devices are 32-bit elements; how exact they have to be, the bound alone decides.
No kernel may reach another device: no remote copies, remote signals or barrier semaphores. Data moves between devices by JAX's collectives and lax.ppermute only.
A program may use at most 128 MiB of HBM per device.

v0:
```python
import jax
import jax.numpy as jnp
from jax import lax
from jax.sharding import PartitionSpec as P

NC = 8192
PANELS = 4
CHILDREN = 4
CAPC = 2
ROT_BITS = 4
RTD = 8


def shifted(value, axis, by):
    count = lax.axis_size(axis)
    return lax.ppermute(value, axis, [(i, (i + by) % count) for i in range(count)])


def padded_to(lines, count):
    spare = -lines.shape[0] % count
    if not spare:
        return lines
    return jnp.concatenate([lines, jnp.zeros((spare, *lines.shape[1:]), lines.dtype)])


def from_root(value, axis, root):
    lines = jnp.where(lax.axis_index(axis) == root, value, jnp.zeros_like(value)).reshape(
        -1, *value.shape[1:][-1:]
    )
    padded = padded_to(lines, lax.axis_size(axis))
    own = lax.psum_scatter(padded, axis, scatter_dimension=0, tiled=True)
    return lax.all_gather(own, axis, axis=0, tiled=True)[: len(lines)].reshape(value.shape)


def shards(child_tiles, tile_dest, tile_counts, child_offsets):
    row_count = lax.axis_size("row")
    col_count = lax.axis_size("col")
    row_here = lax.axis_index("row")
    col_here = lax.axis_index("col")
    slot_count = child_tiles.shape[0]
    tile_size = child_tiles.shape[1]
    cols_local = NC // col_count
    tiles_col = cols_local // tile_size
    highest = lax.Precision.HIGHEST
    count_here = tile_counts[0, 0]
    slot_ids = jnp.arange(slot_count, dtype=jnp.int32)
    live_mask = slot_ids < count_here
    child_here = col_here // (col_count // CHILDREN)
    offset_here = jnp.sum(jnp.where(jnp.arange(CHILDREN) == child_here, child_offsets, 0))
    owner_col = tile_dest[:, 0] // tiles_col
    local_col = tile_dest[:, 0] % tiles_col
    local_row = tile_dest[:, 1] + (offset_here + row_here) // row_count
    position = local_row * tiles_col + local_col
    owner_dest = jnp.where(live_mask, owner_col, -1)
    metadata = jnp.stack([owner_dest, position], axis=1)
    amount = offset_here % row_count
    moved_tiles = child_tiles
    moved_meta = metadata
    for bit_index in range(ROT_BITS):
        shifted_tiles, shifted_meta = shifted((moved_tiles, moved_meta), "row", 1 << bit_index)
        take_bit = amount >> bit_index & 1 == 1
        moved_tiles = jnp.where(take_bit, shifted_tiles, moved_tiles)
        moved_meta = jnp.where(take_bit, shifted_meta, moved_meta)
    owner_ids = moved_meta[:, 0]
    owner_hits = (owner_ids[:, None] == jnp.arange(col_count)[None, :]).astype(jnp.int32)
    owner_rank = jnp.sum((jnp.cumsum(owner_hits, axis=0) - 1) * owner_hits, axis=1)
    bucket_id = jnp.where(owner_ids >= 0, owner_ids * CAPC + owner_rank, -1)
    picker = (jnp.arange(col_count * CAPC)[:, None] == bucket_id[None, :]).astype(jnp.float32)
    packed = jnp.einsum("bs,sxy->bxy", picker, moved_tiles, precision=highest)
    filled = jnp.sum(picker, axis=1)
    chosen_pos = jnp.sum(jnp.where(picker > 0, moved_meta[None, :, 1], 0), axis=1)
    packed_pos = jnp.where(filled > 0, chosen_pos, -1).astype(jnp.int32)
    packed = packed.reshape(col_count, CAPC, tile_size, tile_size)
    packed_pos = packed_pos.reshape(col_count, CAPC)
    arrived, arrived_pos = (
        lax.all_to_all(packed, "col", split_axis=0, concat_axis=0, tiled=True),
        lax.all_to_all(packed_pos, "col", split_axis=0, concat_axis=0, tiled=True),
    )
    arrived = arrived.reshape(col_count * CAPC, tile_size, tile_size)
    arrived_pos = arrived_pos.reshape(col_count * CAPC)
    placer = (arrived_pos[:, None] == jnp.arange(RTD * tiles_col)[None, :]).astype(jnp.float32)
    placer = placer.reshape(col_count * CAPC, RTD, tiles_col)
    front_local = jnp.einsum("brc,bxy->rxcy", placer, arrived, precision=highest)
    front_local = front_local.reshape(RTD * tile_size, cols_local)
    width = PANELS * tile_size
    col_index = col_here * cols_local + jnp.arange(cols_local)
    leading = from_root(front_local, "col", 0)
    gram_block = jnp.einsum("ri,rj->ij", leading, leading, precision=highest)
    cross_terms = jnp.einsum("ri,rj->ij", leading, front_local, precision=highest)
    gram_block, cross_terms = lax.psum((gram_block, cross_terms), "row")
    lower_factor = jnp.linalg.cholesky(gram_block)
    rows_out = jax.scipy.linalg.solve_triangular(lower_factor, cross_terms, lower=True)
    row_index = jnp.arange(width)
    result = jnp.where(col_index[None, :] >= row_index[:, None], rows_out, jnp.zeros_like(rows_out))
    return result


def solution(mesh):
    return jax.shard_map(
        shards,
        mesh=mesh,
        in_specs=(P(("row", "col"), None, None), P(("row", "col"), None), P("row", "col"), P()),
        out_specs=P(None, "col"),
        check_vma=False,
    )
```

profile of v0, /device:TPU:1, one launch (start us, length us, event | category | flops | bytes accessed | tf_op | source)
XLA Modules:
  0.0 1001.6 jit_solution(12923739866905033209)
XLA Ops:
  6.5 2.5 collective-permute-start.4
  12.2 46.8 %collective-permute-done.4 = f32[8,256,256]{2,1,0:T(8,128)} collective-permute-done((f32[8,256,256]{2,1,0:T(8,128)}, f32[8,256,256]{2,1,0:T(8,128)}, u32[]{:S(2)}, u32[]{:S(2)}) %collective-permute-start.4) | collective-permute-done | bytes 2097184 | tf_op jit(solution)/shard_map/ppermute | solution.py:16
  62.3 48.4 %collective-permute-done.5 = f32[8,256,256]{2,1,0:T(8,128)} collective-permute-done((f32[8,256,256]{2,1,0:T(8,128)S(1)}, f32[8,256,256]{2,1,0:T(8,128)}, u32[]{:S(2)}, u32[]{:S(2)}) %collective-permute-start.5) | collective-permute-done | bytes 2097184 | tf_op jit(solution)/shard_map/ppermute | solution.py:16
  114.1 44.8 %collective-permute-done.6 = f32[8,256,256]{2,1,0:T(8,128)} collective-permute-done((f32[8,256,256]{2,1,0:T(8,128)S(1)}, f32[8,256,256]{2,1,0:T(8,128)}, u32[]{:S(2)}, u32[]{:S(2)}) %collective-permute-start.6) | collective-permute-done | bytes 2097184 | tf_op jit(solution)/shard_map/ppermute | solution.py:16
  161.1 6.1 collective-permute-done.1
  167.2 36.4 %collective-permute-start.2 = (s32[8,2]{0,1:T(2,128)S(1)}, s32[8,2]{0,1:T(2,128)S(1)}, u32[]{:S(2)}, u32[]{:S(2)}) collective-permute-start(s32[8,2]{0,1:T(2,128)S(1)} %broadcast_select_fusion.6), channel_id=1, source_target_pairs={{0,32},{8,40},{16,48},{24,56},{32,64},{40,72},{48,80},{56,88},{64,... | collective-permute-start | bytes 200 | tf_op jit(solution)/shard_map/ppermute | solution.py:16
  203.6 3.0 collective-permute-done.2
  207.0 3.5 collective-permute-done.3
  211.7 10.0 all-to-all-start.1
  221.9 4.0 fusion.15
  225.9 5.8 reshape.158
  231.7 5.7 copy.20
  237.5 4.8 all-to-all-start
  243.8 47.4 %all-to-all-done = f32[8,2,256,256]{3,1,2,0:T(2,128)} async-done(((f32[8,2,256,256]{3,1,2,0:T(2,128)}), f32[8,2,256,256]{3,1,2,0:T(2,128)}, u32[]{:S(2)}, u32[]{:S(2)}) %all-to-all-start) | async-done | bytes 4194336 | tf_op jit(solution)/shard_map/all_to_all | solution.py:76
  291.2 6.6 copy.21
  297.8 6.0 reshape.185
  303.8 8.5 fusion.4
  312.4 10.4 %copy.23 = f32[8,256,4,256]{1,0,3,2:T(8,128)} copy(f32[8,256,4,256]{3,0,2,1:T(8,128)} %fusion.4) | data formatting | bytes 16777216 | tf_op jit(solution)/shard_map/brc,bxy->rxcy/transpose | solution.py:83
  322.8 7.5 copy.28
  330.3 3.2 copy-done
  333.5 4.1 broadcast_select_fusion
  337.7 48.0 %reduce-scatter.2.cloned.1.call-done = f32[256,1024]{0,1:T(8,128)} async-done(((f32[2048,1024]{0,1:T(8,128)}), f32[256,1024]{0,1:T(8,128)}) %reduce-scatter.2.cloned.1.call-update) | async-done | bytes 1048592 | tf_op jit(solution)/shard_map/reduce_scatter | solution.py:31
  386.3 51.4 %all-gather.2.cloned.1.call-done = f32[2048,1024]{0,1:T(8,128)} async-done(((f32[256,1024]{0,1:T(8,128)}), f32[2048,1024]{0,1:T(8,128)}) %all-gather.2.cloned.1.call-update) | async-done | bytes 8388624 | tf_op jit(solution)/shard_map/all_gather | solution.py:32
  437.7 32.7 %fusion.88 = f32[1024,1024]{0,1:T(8,128)} fusion(f32[2048,1024]{0,1:T(8,128)} %all-gather.2.cloned.1.call-done), kind=kOutput, calls=%fused_computation.202 | convolution fusion | flops 25769803776 | bytes 12582912 | tf_op jit(solution)/shard_map/ri,rj->ij/dot_general | solution.py:88
  470.4 35.5 %fusion.89 = f32[1024,1024]{1,0:T(8,128)} fusion(f32[2048,1024]{0,1:T(8,128)S(1)} %copy-done.6, f32[2048,1024]{0,1:T(8,128)} %bitcast.137), kind=kOutput, calls=%fused_computation.203 | convolution fusion | flops 25769803776 | bytes 20971520 | tf_op jit(solution)/shard_map/ri,rj->ij/dot_general | solution.py:89
  506.0 141.6 %all-reduce.4.cloned.1.call-done = (f32[1024,1024]{1,0:T(8,128)}, f32[1024,1024]{0,1:T(8,128)}) async-done(((f32[1024,1024]{1,0:T(8,128)}, f32[1024,1024]{0,1:T(8,128)}), (f32[1024,1024]{1,0:T(8,128)}, f32[1024,1024]{0,1:T(8,128)})) %all-reduce.4.cloned.1.call-update) | async-done | bytes 8388624 | tf_op jit(solution)/shard_map/psum | solution.py:90
  647.6 5.5 copy.25
  653.1 4.4 fusion
  659.5 11.7 %cholesky.223 = f32[128,128]{1,0:T(8,128)S(1)} custom-call(f32[128,128]{1,0:T(8,128)S(1)} %cholesky.580), custom_call_target="Cholesky" | custom-call | tf_op jit(solution)/shard_map/jit(cholesky)/cholesky | solution.py:91
  671.3 2.5 cholesky.255
  673.8 9.8 custom-call.63
  683.6 2.3 constant_dynamic-update-slice_fusion.32
  687.5 11.9 %cholesky.244 = f32[128,128]{1,0:T(8,128)S(1)} custom-call(f32[128,128]{1,0:T(8,128)S(1)} %cholesky.584), custom_call_target="Cholesky" | custom-call | tf_op jit(solution)/shard_map/jit(cholesky)/cholesky | solution.py:91
  700.0 9.8 custom-call.64
  713.2 11.7 %cholesky.468 = f32[128,128]{1,0:T(8,128)S(1)} custom-call(f32[128,128]{1,0:T(8,128)S(1)} %cholesky.589), custom_call_target="Cholesky" | custom-call | tf_op jit(solution)/shard_map/jit(cholesky)/cholesky | solution.py:91
  726.1 9.8 custom-call.65
  737.1 2.3 convolution_subtract_fusion.7
  739.4 12.1 %cholesky.487 = f32[128,128]{1,0:T(8,128)S(1)} custom-call(f32[128,128]{1,0:T(8,128)S(1)} %cholesky.594), custom_call_target="Cholesky" | custom-call | tf_op jit(solution)/shard_map/jit(cholesky)/cholesky | solution.py:91
  752.8 9.8 custom-call.66
  763.7 2.3 convolution_subtract_fusion.8
  766.0 11.7 %cholesky.506 = f32[128,128]{1,0:T(8,128)S(1)} custom-call(f32[128,128]{1,0:T(8,128)S(1)} %cholesky.599), custom_call_target="Cholesky" | custom-call | tf_op jit(solution)/shard_map/jit(cholesky)/cholesky | solution.py:91
  779.0 10.0 custom-call.67
  790.0 2.3 convolution_subtract_fusion.9
  792.3 11.7 %cholesky.526 = f32[128,128]{1,0:T(8,128)S(1)} custom-call(f32[128,128]{1,0:T(8,128)S(1)} %cholesky.604), custom_call_target="Cholesky" | custom-call | tf_op jit(solution)/shard_map/jit(cholesky)/cholesky | solution.py:91
  805.3 9.8 custom-call.68
  818.1 11.9 %cholesky.546 = f32[128,128]{1,0:T(8,128)S(1)} custom-call(f32[128,128]{1,0:T(8,128)S(1)} %cholesky.609), custom_call_target="Cholesky" | custom-call | tf_op jit(solution)/shard_map/jit(cholesky)/cholesky | solution.py:91
  831.2 9.8 custom-call.69
  843.7 11.7 %cholesky.564 = f32[128,128]{1,0:T(8,128)S(1)} custom-call(f32[128,128]{1,0:T(8,128)S(1)} %convolution_subtract_fusion.11), custom_call_target="Cholesky" | custom-call | tf_op jit(solution)/shard_map/jit(cholesky)/cholesky | solution.py:91
  862.2 4.9 select_select_fusion
  867.1 22.8 %while.1 = (s32[]{:T(128)}, f32[1024,1024]{1,0:T(8,128)}, s32[8,2]{0,1:T(2,128)S(1)}, f32[8,128,128]{2,1,0:T(8,128)S(1)}, s32[]{:T(128)}) while((s32[]{:T(128)}, f32[1024,1024]{1,0:T(8,128)}, s32[8,2]{0,1:T(2,128)S(1)}, f32[8,128,128]{2,1,0:T(8,128)S(1)}, s32[]{:T(128)}) %tuple.59), condition=%wide.while_cond, body=%wide.while_body.sunk | while | flops 2 | bytes 131181 | solution.py:92
  867.7 2.2 bitcast_dynamic-update-slice_fusion.2
  870.6 2.2 bitcast_dynamic-update-slice_fusion.2
  873.5 2.2 bitcast_dynamic-update-slice_fusion.2
  876.3 2.2 bitcast_dynamic-update-slice_fusion.2
  879.2 2.2 bitcast_dynamic-update-slice_fusion.2
  882.1 2.2 bitcast_dynamic-update-slice_fusion.2
  884.9 2.2 bitcast_dynamic-update-slice_fusion.2
  887.8 2.2 bitcast_dynamic-update-slice_fusion.2
  890.0 79.0 %custom-call.70 = f32[8,128,128]{1,2,0:T(8,128)S(1)} custom-call(f32[8,128,128]{2,1,0:T(8,128)S(1)} %get-tuple-element.12), custom_call_target="InvertDiagBlocksLowerTriangular" | custom-call | tf_op jit(solution)/shard_map/jit(_solve_triangular)/triangular_solve | solution.py:92
  978.5 2.2 fusion.26
  981.4 2.6 convolution_subtract_fusion.2
  984.8 2.8 convolution_subtract_fusion.1
  988.3 3.5 convolution_subtract_fusion.3
  992.4 2.5 fusion.3
  (115 shorter events, 54.6 us)
Async XLA Ops:
  6.5 52.5 %collective-permute-start.4 = (f32[8,256,256]{2,1,0:T(8,128)}, f32[8,256,256]{2,1,0:T(8,128)}, u32[]{:S(2)}, u32[]{:S(2)}) collective-permute-start(f32[8,256,256]{2,1,0:T(8,128)} %param.4), channel_id=1, source_target_pairs={{0,8},{8,16},{16,24},{24,32},{32,40},{40,48},{48,56},{56,64},{64,7... | collective-permute-start | bytes 6291464 | tf_op jit(solution)/shard_map/ppermute | solution.py:16
  60.9 1.3 copy-start.3
  60.9 53.0 %copy-start.5 = (s32[8,2]{0,1:T(2,128)S(1)}, s32[8,2]{0,1:T(2,128)}, u32[]{:S(2)}) copy-start(s32[8,2]{0,1:T(2,128)} %param.5) | copy-start | bytes 196
  61.0 49.7 %collective-permute-start.5 = (f32[8,256,256]{2,1,0:T(8,128)S(1)}, f32[8,256,256]{2,1,0:T(8,128)}, u32[]{:S(2)}, u32[]{:S(2)}) collective-permute-start(f32[8,256,256]{2,1,0:T(8,128)S(1)} %broadcast_select_fusion.1), channel_id=1, source_target_pairs={{0,16},{8,24},{16,32},{24,40},{32,48},{40,56},{48,64},{56,72},{64,... | collective-permute-start | bytes 6291464 | tf_op jit(solution)/shard_map/ppermute | solution.py:16
  112.6 1.5 copy-start.2
  112.6 46.4 %collective-permute-start.6 = (f32[8,256,256]{2,1,0:T(8,128)S(1)}, f32[8,256,256]{2,1,0:T(8,128)}, u32[]{:S(2)}, u32[]{:S(2)}) collective-permute-start(f32[8,256,256]{2,1,0:T(8,128)S(1)} %broadcast_select_fusion.2), channel_id=1, source_target_pairs={{0,32},{8,40},{16,48},{24,56},{32,64},{40,72},{48,80},{56,88},{64,... | collective-permute-start | bytes 6291464 | tf_op jit(solution)/shard_map/ppermute | solution.py:16
  114.0 47.0 %collective-permute-start = (s32[8,2]{0,1:T(2,128)S(1)}, s32[8,2]{0,1:T(2,128)S(1)}, u32[]{:S(2)}, u32[]{:S(2)}) collective-permute-start(s32[8,2]{0,1:T(2,128)S(1)} %pad_add_fusion), channel_id=1, source_target_pairs={{0,8},{8,16},{16,24},{24,32},{32,40},{40,48},{48,56},{56,64},{64,7... | collective-permute-start | bytes 200 | tf_op jit(solution)/shard_map/ppermute | solution.py:16
  160.9 60.8 %collective-permute-start.7 = (f32[8,256,256]{2,1,0:T(8,128)S(1)}, f32[8,256,256]{2,1,0:T(8,128)}, u32[]{:S(2)}, u32[]{:S(2)}) collective-permute-start(f32[8,256,256]{2,1,0:T(8,128)S(1)} %broadcast_select_fusion.3), channel_id=1, source_target_pairs={{0,64},{8,72},{16,80},{24,88},{32,96},{40,104},{48,112},{56,120},{... | collective-permute-start | bytes 6291464 | tf_op jit(solution)/shard_map/ppermute | solution.py:16
  161.0 6.2 collective-permute-start.1
  167.2 39.3 %collective-permute-start.2 = (s32[8,2]{0,1:T(2,128)S(1)}, s32[8,2]{0,1:T(2,128)S(1)}, u32[]{:S(2)}, u32[]{:S(2)}) collective-permute-start(s32[8,2]{0,1:T(2,128)S(1)} %broadcast_select_fusion.6), channel_id=1, source_target_pairs={{0,32},{8,40},{16,48},{24,56},{32,64},{40,72},{48,80},{56,88},{64,... | collective-permute-start | bytes 200 | tf_op jit(solution)/shard_map/ppermute | solution.py:16
  206.6 3.9 collective-permute-start.3
  211.7 25.8 %all-to-all-start.1 = ((s32[8,1,2]{2,1,0:T(1,128)}), s32[8,1,2]{2,1,0:T(1,128)S(1)}, u32[]{:S(2)}, u32[]{:S(2)}) async-start(s32[8,1,2]{2,1,0:T(1,128)} %bitcast.5), calls=%async_computation.1 | async-start | bytes 8192 | tf_op jit(solution)/shard_map/all_to_all | solution.py:77
  237.5 53.7 %all-to-all-start = ((f32[8,2,256,256]{3,1,2,0:T(2,128)}), f32[8,2,256,256]{3,1,2,0:T(2,128)}, u32[]{:S(2)}, u32[]{:S(2)}) async-start(f32[8,2,256,256]{3,1,2,0:T(2,128)} %copy.20), calls=%async_computation | async-start | bytes 8388608 | tf_op jit(solution)/shard_map/all_to_all | solution.py:76
  242.3 143.4 %reduce-scatter.2.cloned.1.call-start = ((), (), s32[]{:S(2)}) async-start(), calls=%async_computation.3 | async-start | bytes 9437184 | tf_op jit(solution)/shard_map/reduce_scatter | solution.py:31
  330.3 3.2 copy-start
  337.6 100.1 %all-gather.2.cloned.1.call-start = ((), (), s32[]{:S(2)}) async-start(), calls=%async_computation.4 | async-start | bytes 9437184 | tf_op jit(solution)/shard_map/all_gather | solution.py:32
  385.7 261.9 %all-reduce.4.cloned.1.call-start = ((), (), s32[]{:S(2)}) async-start(), calls=%async_computation.5 | async-start | bytes 16777216 | tf_op jit(solution)/shard_map/psum | solution.py:90
  437.7 32.7 %copy-start.6 = (f32[2048,1024]{0,1:T(8,128)S(1)}, f32[2048,1024]{0,1:T(8,128)}, u32[]{:S(2)}) copy-start(f32[2048,1024]{0,1:T(8,128)} %all-gather.2.cloned.1.call-done) | copy-start | bytes 25165828
  657.5 2.0 copy-start.1
  969.0 4.3 copy-start.4
Sparse Core Ops, SparseCore 0:
  337.7 47.9 reduce-scatter.1
  387.4 50.2 all-gather.1
  506.1 141.4 all-reduce.3
where the time goes:
time: 1010 us; the launch traced here: 1000 us
  waiting for transfers between devices  441 us (44%)
  other arithmetic  276 us (27%)
  matrix products  127 us (13%)
  local copies, waits for them, and re-layouts  80.6 us (8%)
  starting transfers between devices  55.3 us (5%)
  between operations  21.9 us (2%)
    another operation x30, other arithmetic, shards(): lower_factor = jnp.linalg.cholesky(gram_block)  172 us
    ppermute x8, waiting for transfers between devices, shifted(): lax.ppermute(value, axis, [(i, (i + by) % count) for i in range(count)])  153 us
    psum x1, waiting for transfers between devices, shards(): gram_block, cross_terms = lax.psum((gram_block, cross_terms), 'row')  142 us
    another operation x3, other arithmetic, shards(): jax.scipy.linalg.solve_triangular(lower_factor, cross_terms, lower=True)  83.9 us
    all_gather x1, waiting for transfers between devices, from_root(): lax.all_gather(own, axis, axis=0, tiled=True)[:len(lines)]  51.4 us
    reduce_scatter x1, waiting for transfers between devices, from_root(): own = lax.psum_scatter(padded, axis, scatter_dimension=0, tiled=True)  48 us
    all_to_all x1, waiting for transfers between devices, shards(): lax.all_to_all(packed, 'col', split_axis=0, concat_axis=0, tiled=True)  47.4 us
    ppermute x8, starting transfers between devices, shifted(): lax.ppermute(value, axis, [(i, (i + by) % count) for i in range(count)])  39.7 us
  transfers between devices with their start and end apart: 13, of which 10 were waited for; matrix products, arithmetic and copies ran while one was open for 2% of the time, Pallas kernels for 0%

commit v1 on v0

--- a/solution.py
+++ b/solution.py
@@ -29,7 +29,9 @@
     )
     padded = padded_to(lines, lax.axis_size(axis))
     own = lax.psum_scatter(padded, axis, scatter_dimension=0, tiled=True)
-    return lax.all_gather(own, axis, axis=0, tiled=True)[: len(lines)].reshape(value.shape)
+    return jnp.concatenate(
+        lax.all_to_all(jnp.stack([own for _ in range(lax.axis_size(axis))]), axis, 0, 0), 0
+    )[: len(lines)].reshape(value.shape)
 
 
 def shards(child_tiles, tile_dest, tile_counts, child_offsets):

time: 1010 us -> 1080 us (1.069)
  blocking collectives: 0 us -> 99 us
  waiting for transfers between devices: 441 us -> 390 us
  matrix products: 127 us -> 143 us
    all_to_all x0 -> x1, blocking collectives: none -> 99 us  [from_root(): lax.all_to_all(jnp.stack([own for _ in range(lax.axis_size(axis))]), axis...]
    all_gather x1 -> x0, waiting for transfers between devices: 51.4 us -> none  [from_root(): lax.all_gather(own, axis, axis=0, tiled=True)[:len(lines)]]
    dot_general x1, matrix products: 35.5 us -> 55.4 us  [shards(): jnp.einsum('ri,rj->ij', leading, front_local, precision=highest)]
    another operation x24 -> x25, local copies, waits for them, and re-layouts: 22.7 us -> 23.8 us
  transfers between devices with their start and end apart: 13 -> 12, of which waited for: 10 -> 9; matrix products, arithmetic and copies ran while one was open for 2% -> 2% of each run, Pallas kernels for 0% -> 0%
where the time goes in v1:
time: 1080 us; the launch traced here: 1070 us
  waiting for transfers between devices  390 us (36%)
  other arithmetic  276 us (26%)
  matrix products  143 us (13%)
  blocking collectives  99 us (9%)
  local copies, waits for them, and re-layouts  83.1 us (8%)
  starting transfers between devices  54.7 us (5%)
  between operations  22.3 us (2%)
    another operation x30, other arithmetic, shards(): lower_factor = jnp.linalg.cholesky(gram_block)  172 us
    ppermute x8, waiting for transfers between devices, shifted(): lax.ppermute(value, axis, [(i, (i + by) % count) for i in range(count)])  153 us
    psum x1, waiting for transfers between devices, shards(): gram_block, cross_terms = lax.psum((gram_block, cross_terms), 'row')  142 us
    all_to_all x1, blocking collectives, from_root(): lax.all_to_all(jnp.stack([own for _ in range(lax.axis_size(axis))]), axis...  99 us
    another operation x3, other arithmetic, shards(): jax.scipy.linalg.solve_triangular(lower_factor, cross_terms, lower=True)  83.7 us
    dot_general x1, matrix products, shards(): jnp.einsum('ri,rj->ij', leading, front_local, precision=highest)  55.4 us
    reduce_scatter x1, waiting for transfers between devices, from_root(): own = lax.psum_scatter(padded, axis, scatter_dimension=0, tiled=True)  48 us
    all_to_all x1, waiting for transfers between devices, shards(): lax.all_to_all(packed, 'col', split_axis=0, concat_axis=0, tiled=True)  47.5 us
  transfers between devices with their start and end apart: 12, of which 9 were waited for; matrix products, arithmetic and copies ran while one was open for 2% of the time, Pallas kernels for 0%

profile of v1, /device:TPU:1, one launch (start us, length us, event | category | flops | bytes accessed | tf_op | source)
XLA Modules:
  0.0 1067.5 jit_solution(5512942861937777596)
XLA Ops:
  6.5 2.5 collective-permute-start.4
  12.2 46.8 %collective-permute-done.4 = f32[8,256,256]{2,1,0:T(8,128)} collective-permute-done((f32[8,256,256]{2,1,0:T(8,128)}, f32[8,256,256]{2,1,0:T(8,128)}, u32[]{:S(2)}, u32[]{:S(2)}) %collective-permute-start.4) | collective-permute-done | bytes 2097184 | tf_op jit(solution)/shard_map/ppermute | solution.py:16
  62.3 48.4 %collective-permute-done.5 = f32[8,256,256]{2,1,0:T(8,128)} collective-permute-done((f32[8,256,256]{2,1,0:T(8,128)S(1)}, f32[8,256,256]{2,1,0:T(8,128)}, u32[]{:S(2)}, u32[]{:S(2)}) %collective-permute-start.5) | collective-permute-done | bytes 2097184 | tf_op jit(solution)/shard_map/ppermute | solution.py:16
  114.1 44.8 %collective-permute-done.6 = f32[8,256,256]{2,1,0:T(8,128)} collective-permute-done((f32[8,256,256]{2,1,0:T(8,128)S(1)}, f32[8,256,256]{2,1,0:T(8,128)}, u32[]{:S(2)}, u32[]{:S(2)}) %collective-permute-start.6) | collective-permute-done | bytes 2097184 | tf_op jit(solution)/shard_map/ppermute | solution.py:16
  161.1 6.1 collective-permute-done.1
  167.2 36.4 %collective-permute-start.2 = (s32[8,2]{0,1:T(2,128)S(1)}, s32[8,2]{0,1:T(2,128)S(1)}, u32[]{:S(2)}, u32[]{:S(2)}) collective-permute-start(s32[8,2]{0,1:T(2,128)S(1)} %broadcast_select_fusion.6), channel_id=1, source_target_pairs={{0,32},{8,40},{16,48},{24,56},{32,64},{40,72},{48,80},{56,88},{64,... | collective-permute-start | bytes 200 | tf_op jit(solution)/shard_map/ppermute | solution.py:16
  203.6 3.0 collective-permute-done.2
  207.0 3.5 collective-permute-done.3
  211.7 10.0 all-to-all-start.1
  221.9 4.0 fusion.15
  225.9 5.8 reshape.163
  231.7 5.7 copy.25
  237.5 4.8 all-to-all-start
  243.7 47.5 %all-to-all-done = f32[8,2,256,256]{3,1,2,0:T(2,128)} async-done(((f32[8,2,256,256]{3,1,2,0:T(2,128)}), f32[8,2,256,256]{3,1,2,0:T(2,128)}, u32[]{:S(2)}, u32[]{:S(2)}) %all-to-all-start) | async-done | bytes 4194336 | tf_op jit(solution)/shard_map/all_to_all | solution.py:78
  291.2 6.6 copy.26
  297.8 6.0 reshape.191
  303.8 8.5 fusion.4
  312.4 10.4 copy.28
  322.8 7.5 copy.37
  330.3 3.2 copy-done
  333.5 4.1 broadcast_select_fusion
  337.7 48.0 %reduce-scatter.2.cloned.1.call-done = f32[256,1024]{0,1:T(8,128)} async-done(((f32[2048,1024]{0,1:T(8,128)}), f32[256,1024]{0,1:T(8,128)}) %reduce-scatter.2.cloned.1.call-update) | async-done | bytes 1048592 | tf_op jit(solution)/shard_map/reduce_scatter | solution.py:31
  388.4 99.0 %all_to_all.16 = f32[8,256,1024]{2,1,0:T(8,128)S(1)} all-to-all(f32[8,256,1024]{2,1,0:T(8,128)S(1)} %stack.5), channel_id=1, replica_groups=mesh['row'=16,'col'=8] {'col'}, dimensions={0} | all-to-all | bytes 16777216 | tf_op jit(solution)/shard_map/all_to_all | solution.py:33
  487.4 55.4 %fusion.88 = f32[1024,1024]{1,0:T(8,128)} fusion(f32[2048,1024]{1,0:T(8,128)S(1)} %bitcast.144, f32[2048,1024]{0,1:T(8,128)S(1)} %bitcast.142), kind=kOutput, calls=%fused_computation.203 | convolution fusion | flops 25769803776 | bytes 20971520 | tf_op jit(solution)/shard_map/ri,rj->ij/dot_general | solution.py:91
  542.7 29.0 %convolution_bitcast_fusion = f32[1024,1024]{0,1:T(8,128)} fusion(f32[8,256,1024]{2,1,0:T(8,128)S(1)} %all_to_all.16), kind=kOutput, calls=%fused_computation.12 | convolution fusion | flops 25769803776 | bytes 12582912 | tf_op jit(solution)/shard_map/ri,rj->ij/dot_general | solution.py:90
  571.8 141.5 %all-reduce.4.cloned.1.call-done = (f32[1024,1024]{1,0:T(8,128)}, f32[1024,1024]{0,1:T(8,128)}) async-done(((f32[1024,1024]{1,0:T(8,128)}, f32[1024,1024]{0,1:T(8,128)}), (f32[1024,1024]{1,0:T(8,128)}, f32[1024,1024]{0,1:T(8,128)})) %all-reduce.4.cloned.1.call-update) | async-done | bytes 8388624 | tf_op jit(solution)/shard_map/psum | solution.py:92
  713.4 5.3 copy.32
  718.7 4.4 fusion
  725.1 11.7 %cholesky.223 = f32[128,128]{1,0:T(8,128)S(1)} custom-call(f32[128,128]{1,0:T(8,128)S(1)} %cholesky.580), custom_call_target="Cholesky" | custom-call | tf_op jit(solution)/shard_map/jit(cholesky)/cholesky | solution.py:93
  736.9 2.5 cholesky.255
  739.4 9.8 custom-call.63
  749.2 2.3 constant_dynamic-update-slice_fusion.32
  753.1 11.9 %cholesky.244 = f32[128,128]{1,0:T(8,128)S(1)} custom-call(f32[128,128]{1,0:T(8,128)S(1)} %cholesky.584), custom_call_target="Cholesky" | custom-call | tf_op jit(solution)/shard_map/jit(cholesky)/cholesky | solution.py:93
  765.6 9.8 custom-call.64
  778.7 11.7 %cholesky.468 = f32[128,128]{1,0:T(8,128)S(1)} custom-call(f32[128,128]{1,0:T(8,128)S(1)} %cholesky.589), custom_call_target="Cholesky" | custom-call | tf_op jit(solution)/shard_map/jit(cholesky)/cholesky | solution.py:93
  791.7 9.8 custom-call.65
  802.6 2.3 convolution_subtract_fusion.7
  805.0 11.9 %cholesky.487 = f32[128,128]{1,0:T(8,128)S(1)} custom-call(f32[128,128]{1,0:T(8,128)S(1)} %cholesky.594), custom_call_target="Cholesky" | custom-call | tf_op jit(solution)/shard_map/jit(cholesky)/cholesky | solution.py:93
  818.2 9.8 custom-call.66
  829.1 2.3 convolution_subtract_fusion.8
  831.4 11.7 %cholesky.506 = f32[128,128]{1,0:T(8,128)S(1)} custom-call(f32[128,128]{1,0:T(8,128)S(1)} %cholesky.599), custom_call_target="Cholesky" | custom-call | tf_op jit(solution)/shard_map/jit(cholesky)/cholesky | solution.py:93
  844.4 10.2 custom-call.67
  855.6 2.3 convolution_subtract_fusion.9
  857.9 11.7 %cholesky.526 = f32[128,128]{1,0:T(8,128)S(1)} custom-call(f32[128,128]{1,0:T(8,128)S(1)} %cholesky.604), custom_call_target="Cholesky" | custom-call | tf_op jit(solution)/shard_map/jit(cholesky)/cholesky | solution.py:93
  870.9 9.8 custom-call.68
  883.7 11.9 %cholesky.546 = f32[128,128]{1,0:T(8,128)S(1)} custom-call(f32[128,128]{1,0:T(8,128)S(1)} %cholesky.609), custom_call_target="Cholesky" | custom-call | tf_op jit(solution)/shard_map/jit(cholesky)/cholesky | solution.py:93
  896.8 9.8 custom-call.69
  909.2 11.7 %cholesky.564 = f32[128,128]{1,0:T(8,128)S(1)} custom-call(f32[128,128]{1,0:T(8,128)S(1)} %convolution_subtract_fusion.11), custom_call_target="Cholesky" | custom-call | tf_op jit(solution)/shard_map/jit(cholesky)/cholesky | solution.py:93
  927.8 4.9 select_select_fusion
  932.7 22.8 %while.1 = (s32[]{:T(128)}, f32[1024,1024]{1,0:T(8,128)}, s32[8,2]{0,1:T(2,128)S(1)}, f32[8,128,128]{2,1,0:T(8,128)S(1)}, s32[]{:T(128)}) while((s32[]{:T(128)}, f32[1024,1024]{1,0:T(8,128)}, s32[8,2]{0,1:T(2,128)S(1)}, f32[8,128,128]{2,1,0:T(8,128)S(1)}, s32[]{:T(128)}) %tuple.59), condition=%wide.while_cond, body=%wide.while_body.sunk | while | flops 2 | bytes 131181 | solution.py:94
  933.3 2.2 bitcast_dynamic-update-slice_fusion.2
  936.2 2.2 bitcast_dynamic-update-slice_fusion.2
  939.1 2.2 bitcast_dynamic-update-slice_fusion.2
  941.9 2.2 bitcast_dynamic-update-slice_fusion.2
  944.8 2.2 bitcast_dynamic-update-slice_fusion.2
  947.6 2.2 bitcast_dynamic-update-slice_fusion.2
  950.5 2.2 bitcast_dynamic-update-slice_fusion.2
  953.4 2.2 bitcast_dynamic-update-slice_fusion.2
  955.5 78.8 %custom-call.70 = f32[8,128,128]{1,2,0:T(8,128)S(1)} custom-call(f32[8,128,128]{2,1,0:T(8,128)S(1)} %get-tuple-element.12), custom_call_target="InvertDiagBlocksLowerTriangular" | custom-call | tf_op jit(solution)/shard_map/jit(_solve_triangular)/triangular_solve | solution.py:94
  1043.9 2.2 fusion.26
  1046.8 2.6 convolution_subtract_fusion.2
  1050.1 2.8 convolution_subtract_fusion.1
  1053.6 3.5 convolution_subtract_fusion.3
  1057.8 2.5 fusion.3
  (118 shorter events, 56.5 us)
Async XLA Ops:
  6.5 52.5 %collective-permute-start.4 = (f32[8,256,256]{2,1,0:T(8,128)}, f32[8,256,256]{2,1,0:T(8,128)}, u32[]{:S(2)}, u32[]{:S(2)}) collective-permute-start(f32[8,256,256]{2,1,0:T(8,128)} %param.4), channel_id=1, source_target_pairs={{0,8},{8,16},{16,24},{24,32},{32,40},{40,48},{48,56},{56,64},{64,7... | collective-permute-start | bytes 6291464 | tf_op jit(solution)/shard_map/ppermute | solution.py:16
  60.9 1.3 copy-start.3
  60.9 53.0 %copy-start.5 = (s32[8,2]{0,1:T(2,128)S(1)}, s32[8,2]{0,1:T(2,128)}, u32[]{:S(2)}) copy-start(s32[8,2]{0,1:T(2,128)} %param.5) | copy-start | bytes 196
  61.0 49.7 %collective-permute-start.5 = (f32[8,256,256]{2,1,0:T(8,128)S(1)}, f32[8,256,256]{2,1,0:T(8,128)}, u32[]{:S(2)}, u32[]{:S(2)}) collective-permute-start(f32[8,256,256]{2,1,0:T(8,128)S(1)} %broadcast_select_fusion.1), channel_id=1, source_target_pairs={{0,16},{8,24},{16,32},{24,40},{32,48},{40,56},{48,64},{56,72},{64,... | collective-permute-start | bytes 6291464 | tf_op jit(solution)/shard_map/ppermute | solution.py:16
  112.6 1.5 copy-start.2
  112.6 46.4 %collective-permute-start.6 = (f32[8,256,256]{2,1,0:T(8,128)S(1)}, f32[8,256,256]{2,1,0:T(8,128)}, u32[]{:S(2)}, u32[]{:S(2)}) collective-permute-start(f32[8,256,256]{2,1,0:T(8,128)S(1)} %broadcast_select_fusion.2), channel_id=1, source_target_pairs={{0,32},{8,40},{16,48},{24,56},{32,64},{40,72},{48,80},{56,88},{64,... | collective-permute-start | bytes 6291464 | tf_op jit(solution)/shard_map/ppermute | solution.py:16
  114.0 47.0 %collective-permute-start = (s32[8,2]{0,1:T(2,128)S(1)}, s32[8,2]{0,1:T(2,128)S(1)}, u32[]{:S(2)}, u32[]{:S(2)}) collective-permute-start(s32[8,2]{0,1:T(2,128)S(1)} %pad_add_fusion), channel_id=1, source_target_pairs={{0,8},{8,16},{16,24},{24,32},{32,40},{40,48},{48,56},{56,64},{64,7... | collective-permute-start | bytes 200 | tf_op jit(solution)/shard_map/ppermute | solution.py:16
  160.9 60.8 %collective-permute-start.7 = (f32[8,256,256]{2,1,0:T(8,128)S(1)}, f32[8,256,256]{2,1,0:T(8,128)}, u32[]{:S(2)}, u32[]{:S(2)}) collective-permute-start(f32[8,256,256]{2,1,0:T(8,128)S(1)} %broadcast_select_fusion.3), channel_id=1, source_target_pairs={{0,64},{8,72},{16,80},{24,88},{32,96},{40,104},{48,112},{56,120},{... | collective-permute-start | bytes 6291464 | tf_op jit(solution)/shard_map/ppermute | solution.py:16
  161.0 6.2 collective-permute-start.1
  167.2 39.3 %collective-permute-start.2 = (s32[8,2]{0,1:T(2,128)S(1)}, s32[8,2]{0,1:T(2,128)S(1)}, u32[]{:S(2)}, u32[]{:S(2)}) collective-permute-start(s32[8,2]{0,1:T(2,128)S(1)} %broadcast_select_fusion.6), channel_id=1, source_target_pairs={{0,32},{8,40},{16,48},{24,56},{32,64},{40,72},{48,80},{56,88},{64,... | collective-permute-start | bytes 200 | tf_op jit(solution)/shard_map/ppermute | solution.py:16
  206.6 3.9 collective-permute-start.3
  211.7 25.8 %all-to-all-start.1 = ((s32[8,1,2]{2,1,0:T(1,128)}), s32[8,1,2]{2,1,0:T(1,128)S(1)}, u32[]{:S(2)}, u32[]{:S(2)}) async-start(s32[8,1,2]{2,1,0:T(1,128)} %bitcast.5), calls=%async_computation.1 | async-start | bytes 8192 | tf_op jit(solution)/shard_map/all_to_all | solution.py:79
  237.5 53.7 %all-to-all-start = ((f32[8,2,256,256]{3,1,2,0:T(2,128)}), f32[8,2,256,256]{3,1,2,0:T(2,128)}, u32[]{:S(2)}, u32[]{:S(2)}) async-start(f32[8,2,256,256]{3,1,2,0:T(2,128)} %copy.25), calls=%async_computation | async-start | bytes 8388608 | tf_op jit(solution)/shard_map/all_to_all | solution.py:78
  242.3 143.4 %reduce-scatter.2.cloned.1.call-start = ((), (), s32[]{:S(2)}) async-start(), calls=%async_computation.4 | async-start | bytes 9437184 | tf_op jit(solution)/shard_map/reduce_scatter | solution.py:31
  330.3 3.2 copy-start
  337.6 375.7 %all-reduce.4.cloned.1.call-start = ((), (), s32[]{:S(2)}) async-start(), calls=%async_computation.5 | async-start | bytes 16777216 | tf_op jit(solution)/shard_map/psum | solution.py:92
  387.3 100.1 %slice-start = ((s8[8388608]{0:T(1024)(128)(4,1)}), s8[4194304]{0:T(1024)(128)(4,1)S(1)}, s32[]{:S(2)}) async-start(s8[8388608]{0:T(1024)(128)(4,1)} %bitcast.140), calls=%async_computation.6 | async-start | bytes 8388608
  388.4 99.0 %slice-start.1 = ((s8[8388608]{0:T(1024)(128)(4,1)}), s8[4194304]{0:T(1024)(128)(4,1)S(1)}, s32[]{:S(2)}) async-start(s8[8388608]{0:T(1024)(128)(4,1)} %bitcast.140), calls=%async_computation.7 | async-start | bytes 8388608
  723.1 2.0 copy-start.1
  1034.4 4.3 copy-start.4
Sparse Core Ops, SparseCore 0:
  337.7 47.9 reduce-scatter.1
  571.9 141.3 all-reduce.3
